TPU v7x, 256 devices: a whole 4x4x8 slice. The times are simulated.
256 devices in a mesh: ia: 32 (over z, x_lo, core), ja: 4 (over y), ka: 2 (over x_hi).
Axes of the slice: x: 4 (x_hi: 2, x_lo: 2; x = x_hi * 2 + x_lo), y: 4, z: 8, core: 2. Of those that a mesh axis runs over, the one named last changes fastest.
Arguments:
- tensor: float32 [8192, 8, 8192], P('ja', 'ka', 'ia'), may hold values from -6 to 6
- factor_a: float32 [8192, 128], P('ia'), may hold values from -1 to 1
- factor_c: float32 [8, 128], P('ka'), may hold values from -2 to 2
- gram_c: float32 [128, 128], replicated, may hold values from -12 to 24, as said below
Outputs:
- factor_b: float32 [8192, 128], P('ja')
- factor_c_new: float32 [8, 128], P('ka')
Inputs may be any that keep to these rules, and one draw needn't show every extreme that they name: `gram_c`: symmetric positive definite.
All inputs are finite; a program needn't handle non-finite values.
Results may differ from a plain program's by a relative error of at most 0.000071.
Values sent between devices are 32-bit elements; how exact they have to be, the bound alone decides.
No kernel may reach another device: no remote copies, remote signals or barrier semaphores. Data moves between devices by JAX's collectives and lax.ppermute only.
A program may use at most 64 MiB of HBM per device.

v0:
```python
import jax
import jax.numpy as jnp
from jax import lax
from jax.sharding import PartitionSpec as P


def right_solve(rhs, system):
    lower = jnp.linalg.cholesky(system)
    middle = lax.linalg.triangular_solve(lower, rhs, left_side=False, lower=True, transpose_a=True)
    return lax.linalg.triangular_solve(
        lower, middle, left_side=False, lower=True, transpose_a=False
    )


def body(tensor, factor_a, factor_c, gram_c):
    high = lax.Precision.HIGHEST
    mode_two, mode_three, mode_one = tensor.shape
    rank = factor_a.shape[1]
    gram_a = lax.psum(
        jnp.dot(factor_a.T, factor_a, precision=high, preferred_element_type=jnp.float32), "ia"
    )
    system_b = gram_a * gram_c
    count = mode_two // lax.axis_size("ia") * lax.axis_size("ia")
    flat = jnp.dot(
        tensor.reshape(count * mode_three, mode_one),
        factor_a,
        precision=high,
        preferred_element_type=jnp.float32,
    )
    shares = lax.psum_scatter(
        flat.reshape(count, mode_three, rank), "ia", scatter_dimension=0, tiled=True
    )
    local_b = lax.psum(jnp.sum(shares * factor_c[None, :, :], axis=1), "ka")
    rows_b = right_solve(local_b, system_b)
    local_c = jnp.sum(shares * rows_b[:, None, :], axis=0)
    local_gram = jnp.dot(rows_b.T, rows_b, precision=high, preferred_element_type=jnp.float32)
    mttkrp_c, gram_b = lax.psum((local_c, local_gram), ("ia", "ja"))
    factor_b = lax.all_gather(rows_b, "ia", axis=0, tiled=True)
    factor_c_new = right_solve(mttkrp_c, gram_a * gram_b)
    return (factor_b, factor_c_new)


def solution(mesh):
    placed = (P("ja", "ka", "ia"), P("ia", None), P("ka", None), P())
    return jax.shard_map(
        body, mesh=mesh, in_specs=placed, out_specs=(P("ja", None), P("ka", None)), check_vma=False
    )
```

profile of v0, /device:TPU:1, one launch (start us, length us, event | category | flops | bytes accessed | tf_op | source)
XLA Modules:
  0.0 1342.1 jit_solution(12914689093623090301)
XLA Ops:
  7.2 0.8 copy-done
  8.1 1.0 fusion.15
  9.2 11.6 fusion
  20.9 186.3 %all-reduce.3.cloned.1.call-done = f32[128,128]{0,1:T(8,128)} async-done(((f32[128,128]{0,1:T(8,128)}), f32[128,128]{0,1:T(8,128)}) %all-reduce.3.cloned.1.call-update) | async-done | bytes 65552 | tf_op jit(solution)/shard_map/psum | solution.py:19
  207.2 0.8 mul.24
  208.2 11.7 cholesky.44
  220.0 0.6 compare_reduce_fusion.1
  220.6 0.7 fusion.3
  221.3 9.8 custom-call.12
  231.1 97.8 %reduce-scatter.2.cloned.1.call-done = f32[64,4,128]{2,0,1:T(8,128)} async-done(((f32[2048,4,128]{2,0,1:T(8,128)}), f32[64,4,128]{2,0,1:T(8,128)}) %reduce-scatter.2.cloned.1.call-update) | async-done | bytes 131088 | tf_op jit(solution)/shard_map/reduce_scatter | solution.py:30
  328.9 0.9 multiply_reduce_fusion.1
  329.9 9.2 psum.28
  339.5 0.9 fusion.16
  341.0 0.9 multiply_reduce_fusion
  341.9 277.2 %psum.30 = f32[4,128]{1,0:T(4,128)S(1)} all-reduce(f32[4,128]{1,0:T(4,128)S(1)} %multiply_reduce_fusion), channel_id=1, replica_groups=mesh['ia'=32,'ja'=4,'ka'=2] {'ia','ja'}, use_global_device_ids=true, to_apply=%region_7.9 | all-reduce | flops 512 | bytes 4096 | tf_op jit(solution)/shard_map/psum | solution.py:37
  619.1 650.4 %all-reduce.5.cloned.1.call-done = f32[128,128]{0,1:T(8,128)} async-done(((f32[128,128]{0,1:T(8,128)}), f32[128,128]{0,1:T(8,128)}) %all-reduce.5.cloned.1.call-update) | async-done | bytes 65552 | tf_op jit(solution)/shard_map/psum | solution.py:37
  1269.6 0.9 mul.27
  1270.6 11.7 cholesky.55
  1282.3 0.6 compare_reduce_fusion
  1282.9 0.7 fusion.4
  1283.6 9.8 custom-call.13
  1293.6 0.8 fusion.5
  1294.4 38.9 %all-gather.2.cloned.1.call-done = f32[2048,128]{1,0:T(8,128)} async-done(((f32[64,128]{1,0:T(8,128)}), f32[2048,128]{1,0:T(8,128)}) %all-gather.2.cloned.1.call-update) | async-done | bytes 1048592 | tf_op jit(solution)/shard_map/all_gather | solution.py:38
  1333.3 2.3 copy.19
  (25 shorter events, 1.7 us)
Async XLA Ops:
  7.2 0.9 copy-start
  7.2 200.1 %all-reduce.3.cloned.1.call-start = ((), (), s32[]{:S(2)}) async-start(), calls=%async_computation.2 | async-start | bytes 131072 | tf_op jit(solution)/shard_map/psum | solution.py:19
  9.1 11.7 copy-start.2
  9.1 319.8 %copy-start.3 = (f32[4,128]{1,0:T(4,128)S(1)}, f32[4,128]{1,0:T(4,128)}, u32[]{:S(2)}) copy-start(f32[4,128]{1,0:T(4,128)} %param.7) | copy-start | bytes 6148
  9.1 319.8 %reduce-scatter.2.cloned.1.call-start = ((), (), s32[]{:S(2)}) async-start(), calls=%async_computation.1 | async-start | bytes 4325376 | tf_op jit(solution)/shard_map/reduce_scatter | solution.py:30
  20.8 1248.8 %all-reduce.5.cloned.1.call-start = ((), (), s32[]{:S(2)}) async-start(), calls=%async_computation.4 | async-start | bytes 131072 | tf_op jit(solution)/shard_map/psum | solution.py:37
  339.5 1.0 copy-start.1
  340.4 992.9 %all-gather.2.cloned.1.call-start = ((), (), s32[]{:S(2)}) async-start(), calls=%async_computation.3 | async-start | bytes 1081344 | tf_op jit(solution)/shard_map/all_gather | solution.py:38
Sparse Core Ops, SparseCore 0:
  11.2 195.9 all-reduce.2
  209.9 118.9 reduce-scatter.1
  340.5 928.9 all-reduce.4
  1271.3 61.9 all-gather.1
where the time goes:
time: 1340 us
  waiting for transfers between devices  974 us (73%)
  blocking collectives  286 us (21%)
  other arithmetic  49.3 us (4%)
  matrix products  14.9 us (1%)
  between operations  13.9 us (1%)
    psum x1, waiting for transfers between devices, body(): mttkrp_c, gram_b = lax.psum((local_c, local_gram), ('ia', 'ja'))  650 us
    psum x1, blocking collectives, body(): mttkrp_c, gram_b = lax.psum((local_c, local_gram), ('ia', 'ja'))  277 us
    psum x1, waiting for transfers between devices, body(): lax.psum(jnp.dot(factor_a.T, factor_a, precision=high, preferred_element_...  186 us
    reduce_scatter x1, waiting for transfers between devices, body(): lax.psum_scatter(flat.reshape(count, mode_three, rank), 'ia', scatter_dim...  97.8 us
    all_gather x1, waiting for transfers between devices, body(): factor_b = lax.all_gather(rows_b, 'ia', axis=0, tiled=True)  38.9 us
  transfers between devices with their start and end apart: 4, of which 4 were waited for; matrix products, arithmetic and copies ran while one was open for 5% of the time, Pallas kernels for 0%

commit v1 on v0

--- a/solution.py
+++ b/solution.py
@@ -16,9 +16,8 @@
     high = lax.Precision.HIGHEST
     mode_two, mode_three, mode_one = tensor.shape
     rank = factor_a.shape[1]
-    gram_a = lax.psum(
-        jnp.dot(factor_a.T, factor_a, precision=high, preferred_element_type=jnp.float32), "ia"
-    )
+    state = jnp.dot(factor_a.T, factor_a, precision=high, preferred_element_type=jnp.float32)
+    gram_a = lax.all_gather(state, "ia").sum(axis=0)
     system_b = gram_a * gram_c
     count = mode_two // lax.axis_size("ia") * lax.axis_size("ia")
     flat = jnp.dot(

time: 1340 us -> 1210 us (0.903)
  waiting for transfers between devices: 974 us -> 846 us
    psum x1 -> x0, waiting for transfers between devices: 186 us -> none  [body(): lax.psum(jnp.dot(factor_a.T, factor_a, precision=high, preferred_element_...]
    all_gather x0 -> x1, waiting for transfers between devices: none -> 58.4 us  [body(): gram_a = lax.all_gather(state, 'ia').sum(axis=0)]
where the time goes in v1:
time: 1210 us
  waiting for transfers between devices  846 us (70%)
  blocking collectives  285 us (24%)
  other arithmetic  50.1 us (4%)
  matrix products  14.9 us (1%)
  between operations  13.9 us (1%)
    psum x1, waiting for transfers between devices, body(): mttkrp_c, gram_b = lax.psum((local_c, local_gram), ('ia', 'ja'))  651 us
    psum x1, blocking collectives, body(): mttkrp_c, gram_b = lax.psum((local_c, local_gram), ('ia', 'ja'))  277 us
    reduce_scatter x1, waiting for transfers between devices, body(): lax.psum_scatter(flat.reshape(count, mode_three, rank), 'ia', scatter_dim...  97.1 us
    all_gather x1, waiting for transfers between devices, body(): gram_a = lax.all_gather(state, 'ia').sum(axis=0)  58.4 us
    all_gather x1, waiting for transfers between devices, body(): factor_b = lax.all_gather(rows_b, 'ia', axis=0, tiled=True)  39.1 us
    another operation x6, other arithmetic, right_solve(): lower = jnp.linalg.cholesky(system)  24.8 us
  transfers between devices with their start and end apart: 4, of which 4 were waited for; matrix products, arithmetic and copies ran while one was open for 5% of the time, Pallas kernels for 0%

profile of v1, /device:TPU:1, one launch (start us, length us, event | category | flops | bytes accessed | tf_op | source)
XLA Modules:
  0.0 1214.0 jit_solution(15304994901041612694)
XLA Ops:
  7.2 0.8 copy-done
  8.1 1.0 fusion.15
  9.2 11.6 fusion
  20.9 58.4 %all-gather.6.cloned.1.call-done = f32[4096,128]{1,0:T(8,128)} async-done(((f32[128,128]{1,0:T(8,128)}), f32[4096,128]{1,0:T(8,128)}) %all-gather.6.cloned.1.call-update) | async-done | bytes 2097168 | tf_op jit(solution)/shard_map/all_gather | solution.py:20
  79.4 1.7 reduce_sum.28
  81.3 11.7 cholesky.44
  93.0 0.6 compare_reduce_fusion.1
  93.7 0.7 fusion.3
  94.3 9.8 custom-call.12
  104.2 97.1 %reduce-scatter.2.cloned.1.call-done = f32[64,4,128]{2,0,1:T(8,128)} async-done(((f32[2048,4,128]{2,0,1:T(8,128)}), f32[64,4,128]{2,0,1:T(8,128)}) %reduce-scatter.2.cloned.1.call-update) | async-done | bytes 131088 | tf_op jit(solution)/shard_map/reduce_scatter | solution.py:29
  201.2 0.9 multiply_reduce_fusion.1
  202.2 8.6 psum.21
  211.2 0.9 fusion.16
  212.7 0.9 multiply_reduce_fusion
  213.6 276.9 %psum.22 = f32[4,128]{1,0:T(4,128)S(1)} all-reduce(f32[4,128]{1,0:T(4,128)S(1)} %multiply_reduce_fusion), channel_id=1, replica_groups=mesh['ia'=32,'ja'=4,'ka'=2] {'ia','ja'}, use_global_device_ids=true, to_apply=%region_7.9 | all-reduce | flops 512 | bytes 4096 | tf_op jit(solution)/shard_map/psum | solution.py:36
  490.5 650.7 %all-reduce.2.cloned.1.call-done = f32[128,128]{0,1:T(8,128)} async-done(((f32[128,128]{0,1:T(8,128)}), f32[128,128]{0,1:T(8,128)}) %all-reduce.2.cloned.1.call-update) | async-done | bytes 65552 | tf_op jit(solution)/shard_map/psum | solution.py:36
  1141.2 0.8 mul.27
  1142.2 11.7 cholesky.55
  1153.9 0.6 compare_reduce_fusion
  1154.6 0.7 fusion.4
  1155.2 9.8 custom-call.13
  1165.2 0.8 fusion.5
  1166.0 39.1 %all-gather.4.cloned.1.call-done = f32[2048,128]{1,0:T(8,128)} async-done(((f32[64,128]{1,0:T(8,128)}), f32[2048,128]{1,0:T(8,128)}) %all-gather.4.cloned.1.call-update) | async-done | bytes 1048592 | tf_op jit(solution)/shard_map/all_gather | solution.py:37
  1205.2 2.3 copy.23
  (27 shorter events, 1.8 us)
Async XLA Ops:
  7.2 0.9 copy-start
  7.2 72.2 %all-gather.6.cloned.1.call-start = ((), (), s32[]{:S(2)}) async-start(), calls=%async_computation.4 | async-start | bytes 2162688 | tf_op jit(solution)/shard_map/all_gather | solution.py:20
  9.1 11.7 copy-start.2
  9.1 192.1 %copy-start.3 = (f32[4,128]{1,0:T(4,128)S(1)}, f32[4,128]{1,0:T(4,128)}, u32[]{:S(2)}) copy-start(f32[4,128]{1,0:T(4,128)} %param.7) | copy-start | bytes 6148
  9.1 192.1 %reduce-scatter.2.cloned.1.call-start = ((), (), s32[]{:S(2)}) async-start(), calls=%async_computation.1 | async-start | bytes 4325376 | tf_op jit(solution)/shard_map/reduce_scatter | solution.py:29
  20.8 1120.4 %all-reduce.2.cloned.1.call-start = ((), (), s32[]{:S(2)}) async-start(), calls=%async_computation.3 | async-start | bytes 131072 | tf_op jit(solution)/shard_map/psum | solution.py:36
  211.2 1.0 copy-start.1
  212.1 993.0 %all-gather.4.cloned.1.call-start = ((), (), s32[]{:S(2)}) async-start(), calls=%async_computation.2 | async-start | bytes 1081344 | tf_op jit(solution)/shard_map/all_gather | solution.py:37
Sparse Core Ops, SparseCore 0:
  10.4 68.8 all-gather.5
  81.9 119.3 reduce-scatter.1
  212.2 928.9 all-reduce.1
  1143.1 62.0 all-gather.3

commit v2 on v0

--- a/solution.py
+++ b/solution.py
@@ -2,6 +2,7 @@
 import jax.numpy as jnp
 from jax import lax
 from jax.sharding import PartitionSpec as P
+from jax.lax import psum
 
 
 def right_solve(rhs, system):
@@ -34,7 +35,7 @@
     rows_b = right_solve(local_b, system_b)
     local_c = jnp.sum(shares * rows_b[:, None, :], axis=0)
     local_gram = jnp.dot(rows_b.T, rows_b, precision=high, preferred_element_type=jnp.float32)
-    mttkrp_c, gram_b = lax.psum((local_c, local_gram), ("ia", "ja"))
+    mttkrp_c, gram_b = psum(psum((local_c, local_gram), "ja"), "ia")
     factor_b = lax.all_gather(rows_b, "ia", axis=0, tiled=True)
     factor_c_new = right_solve(mttkrp_c, gram_a * gram_b)
     return (factor_b, factor_c_new)

time: 1340 us -> 658 us (0.49)
  waiting for transfers between devices: 974 us -> 502 us
  blocking collectives: 286 us -> 74.1 us
    psum x1 -> x2, waiting for transfers between devices: 650 us -> 176 us  [body(): mttkrp_c, gram_b = psum(psum((local_c, local_gram), 'ja'), 'ia')]
    psum x1 -> x2, blocking collectives: 277 us -> 64.9 us  [body(): mttkrp_c, gram_b = psum(psum((local_c, local_gram), 'ja'), 'ia')]
  transfers between devices with their start and end apart: 4 -> 5, of which waited for: 4 -> 5; matrix products, arithmetic and copies ran while one was open for 5% -> 9% of each run, Pallas kernels for 0% -> 0%
where the time goes in v2:
time: 658 us
  waiting for transfers between devices  502 us (76%)
  blocking collectives  74.1 us (11%)
  other arithmetic  49.3 us (7%)
  matrix products  14.9 us (2%)
  between operations  13.9 us (2%)
    psum x1, waiting for transfers between devices, body(): lax.psum(jnp.dot(factor_a.T, factor_a, precision=high, preferred_element_...  186 us
    psum x2, waiting for transfers between devices, body(): mttkrp_c, gram_b = psum(psum((local_c, local_gram), 'ja'), 'ia')  176 us
    reduce_scatter x1, waiting for transfers between devices, body(): lax.psum_scatter(flat.reshape(count, mode_three, rank), 'ia', scatter_dim...  97.8 us
    psum x2, blocking collectives, body(): mttkrp_c, gram_b = psum(psum((local_c, local_gram), 'ja'), 'ia')  64.9 us
    all_gather x1, waiting for transfers between devices, body(): factor_b = lax.all_gather(rows_b, 'ia', axis=0, tiled=True)  40.8 us
    another operation x6, other arithmetic, right_solve(): lower = jnp.linalg.cholesky(system)  24.8 us
    another operation x4, other arithmetic, right_solve(): lax.linalg.triangular_solve(lower, rhs, left_side=False, lower=True, tran...  20.9 us
  transfers between devices with their start and end apart: 5, of which 5 were waited for; matrix products, arithmetic and copies ran while one was open for 9% of the time, Pallas kernels for 0%

profile of v2, /device:TPU:1, one launch (start us, length us, event | category | flops | bytes accessed | tf_op | source)
XLA Modules:
  0.0 657.8 jit_solution(3539378311613307790)
XLA Ops:
  7.2 0.8 copy-done
  8.1 1.0 fusion.15
  9.2 11.6 %fusion = f32[2048,4,128]{2,0,1:T(8,128)} fusion(f32[2048,4,256]{2,1,0:T(4,128)} %param.5, f32[256,128]{1,0:T(8,128)S(1)} %copy-done), kind=kOutput, calls=%fused_computation | convolution fusion | flops 3221225472 | bytes 12713984 | tf_op jit(solution)/shard_map/dot_general | solution.py:25
  20.9 186.3 %all-reduce.4.cloned.1.call-done = f32[128,128]{0,1:T(8,128)} async-done(((f32[128,128]{0,1:T(8,128)}), f32[128,128]{0,1:T(8,128)}) %all-reduce.4.cloned.1.call-update) | async-done | bytes 65552 | tf_op jit(solution)/shard_map/psum | solution.py:20
  207.2 0.8 mul.24
  208.2 11.7 %cholesky.44 = f32[128,128]{1,0:T(8,128)S(1)} custom-call(f32[128,128]{1,0:T(8,128)S(1)} %fusion.14), custom_call_target="Cholesky" | custom-call | tf_op jit(solution)/shard_map/jit(cholesky)/cholesky | solution.py:9
  220.6 0.7 fusion.3
  221.3 9.8 %custom-call.12 = f32[1,128,128]{1,2,0:T(8,128)S(1)} custom-call(f32[1,128,128]{2,1,0:T(8,128)S(1)} %fusion.3), custom_call_target="InvertDiagBlocksLowerTriangular" | custom-call | tf_op jit(solution)/shard_map/triangular_solve | solution.py:10
  231.1 97.8 %reduce-scatter.2.cloned.1.call-done = f32[64,4,128]{2,0,1:T(8,128)} async-done(((f32[2048,4,128]{2,0,1:T(8,128)}), f32[64,4,128]{2,0,1:T(8,128)}) %reduce-scatter.2.cloned.1.call-update) | async-done | bytes 131088 | tf_op jit(solution)/shard_map/reduce_scatter | solution.py:31
  328.9 0.9 multiply_reduce_fusion.1
  329.9 9.2 %psum.42 = f32[64,128]{1,0:T(8,128)S(1)} all-reduce(f32[64,128]{1,0:T(8,128)S(1)} %multiply_reduce_fusion.1), channel_id=1, replica_groups=mesh['ia'=32,'ja'=4,'ka'=2] {'ka'}, use_global_device_ids=true, to_apply=%region_2.0 | all-reduce | flops 8192 | bytes 65536 | tf_op jit(solution)/shard_map/psum | solution.py:34
  339.5 0.9 fusion.16
  340.5 45.8 %all-reduce.6.cloned.1.call-done = f32[128,128]{0,1:T(8,128)} async-done(((f32[128,128]{0,1:T(8,128)}), f32[128,128]{0,1:T(8,128)}) %all-reduce.6.cloned.1.call-update) | async-done | bytes 65552 | tf_op jit(solution)/shard_map/psum | solution.py:38
  386.9 0.9 multiply_reduce_fusion
  387.8 7.4 %psum.44 = f32[4,128]{1,0:T(4,128)S(1)} all-reduce(f32[4,128]{1,0:T(4,128)S(1)} %multiply_reduce_fusion), channel_id=1, replica_groups=mesh['ia'=32,'ja'=4,'ka'=2] {'ja'}, use_global_device_ids=true, to_apply=%region_7.0 | all-reduce | flops 512 | bytes 4096 | tf_op jit(solution)/shard_map/psum | solution.py:38
  395.2 57.5 %psum.45 = f32[4,128]{1,0:T(4,128)S(1)} all-reduce(f32[4,128]{1,0:T(4,128)S(1)} %psum.44), channel_id=1, replica_groups=mesh['ia'=32,'ja'=4,'ka'=2] {'ia'}, use_global_device_ids=true, to_apply=%region_8.0 | all-reduce | flops 512 | bytes 4096 | tf_op jit(solution)/shard_map/psum | solution.py:38
  452.7 130.7 %all-reduce.8.cloned.1.call-done = f32[128,128]{0,1:T(8,128)} async-done(((f32[128,128]{0,1:T(8,128)}), f32[128,128]{0,1:T(8,128)}) %all-reduce.8.cloned.1.call-update) | async-done | bytes 65552 | tf_op jit(solution)/shard_map/psum | solution.py:38
  583.4 0.9 mul.27
  584.4 11.7 %cholesky.55 = f32[128,128]{1,0:T(8,128)S(1)} custom-call(f32[128,128]{1,0:T(8,128)S(1)} %fusion.9), custom_call_target="Cholesky" | custom-call | tf_op jit(solution)/shard_map/jit(cholesky)/cholesky | solution.py:9
  596.8 0.7 fusion.4
  597.4 9.8 %custom-call.13 = f32[1,128,128]{1,2,0:T(8,128)S(1)} custom-call(f32[1,128,128]{2,1,0:T(8,128)S(1)} %fusion.4), custom_call_target="InvertDiagBlocksLowerTriangular" | custom-call | tf_op jit(solution)/shard_map/triangular_solve | solution.py:10
  607.4 0.8 fusion.5
  608.2 40.8 %all-gather.2.cloned.1.call-done = f32[2048,128]{1,0:T(8,128)} async-done(((f32[64,128]{1,0:T(8,128)}), f32[2048,128]{1,0:T(8,128)}) %all-gather.2.cloned.1.call-update) | async-done | bytes 1048592 | tf_op jit(solution)/shard_map/all_gather | solution.py:39
  649.0 2.3 copy.20
  (29 shorter events, 3.0 us)
Async XLA Ops:
  7.2 0.9 copy-start
  7.2 200.1 %all-reduce.4.cloned.1.call-start = ((), (), s32[]{:S(2)}) async-start(), calls=%async_computation.2 | async-start | bytes 131072 | tf_op jit(solution)/shard_map/psum | solution.py:20
  9.1 11.7 %copy-start.2 = (f32[128,128]{1,0:T(8,128)S(1)}, f32[128,128]{1,0:T(8,128)}, u32[]{:S(2)}) copy-start(f32[128,128]{1,0:T(8,128)} %param.8) | copy-start | bytes 196612
  9.1 319.8 %copy-start.3 = (f32[4,128]{1,0:T(4,128)S(1)}, f32[4,128]{1,0:T(4,128)}, u32[]{:S(2)}) copy-start(f32[4,128]{1,0:T(4,128)} %param.7) | copy-start | bytes 6148
  9.1 319.8 %reduce-scatter.2.cloned.1.call-start = ((), (), s32[]{:S(2)}) async-start(), calls=%async_computation.1 | async-start | bytes 4325376 | tf_op jit(solution)/shard_map/reduce_scatter | solution.py:31
  20.8 365.5 %all-reduce.6.cloned.1.call-start = ((), (), s32[]{:S(2)}) async-start(), calls=%async_computation.4 | async-start | bytes 131072 | tf_op jit(solution)/shard_map/psum | solution.py:38
  339.5 46.9 %copy-start.1 = (f32[64,128]{1,0:T(8,128)}, f32[64,128]{1,0:T(8,128)S(1)}, u32[]{:S(2)}) copy-start(f32[64,128]{1,0:T(8,128)S(1)} %fusion.10) | copy-start | bytes 98308
  340.4 243.0 %all-reduce.8.cloned.1.call-start = ((), (), s32[]{:S(2)}) async-start(), calls=%async_computation.5 | async-start | bytes 131072 | tf_op jit(solution)/shard_map/psum | solution.py:38
  386.3 262.7 %all-gather.2.cloned.1.call-start = ((), (), s32[]{:S(2)}) async-start(), calls=%async_computation.3 | async-start | bytes 1081344 | tf_op jit(solution)/shard_map/all_gather | solution.py:39
Sparse Core Ops, SparseCore 0:
  11.2 195.9 all-reduce.3
  209.9 118.9 reduce-scatter.1
  340.5 45.6 all-reduce.5
  388.7 194.6 all-reduce.7
  585.2 63.7 all-gather.1
